TPU v7x, 32 devices: a whole 2x2x4 slice. The times are simulated.
32 devices in a mesh: expert: 8 (over z, x), dp: 4 (over y, core).
Axes of the slice: x: 2, y: 2, z: 4, core: 2. Of those that a mesh axis runs over, the one named last changes fastest.
Arguments:
- layer_in: bfloat16 [4096, 1024], P(('expert', 'dp')), may hold values from -6 to 6
- routes: int32 [4096, 2], P(('expert', 'dp')), may hold values from 0 to 15, as said below
- queue_slots: int32 [4096, 2], P(('expert', 'dp')), may hold values from -1 to 4, as said below
- norm_attn: float32 [1024], replicated, may hold values from 0.5 to 1.5
- w_query: bfloat16 [1024, 1024], replicated, may hold values from -0.078125 to 0.078125
- w_key: bfloat16 [1024, 1024], replicated, may hold values from -0.078125 to 0.078125
- w_value: bfloat16 [1024, 1024], replicated, may hold values from -0.1875 to 0.1875
- w_out: bfloat16 [1024, 1024], replicated, may hold values from -0.75 to 0.75
- rel_table: float32 [32, 16], replicated, may hold values from -4 to 4
- norm_moe: float32 [1024], replicated, may hold values from 0.5 to 1.5
- router: float32 [1024, 16], replicated, may hold values from -0.375 to 0.375
- w_gate: bfloat16 [16, 1024, 2816], P('expert', None, 'dp'), may hold values from -0.1875 to 0.1875
- w_up: bfloat16 [16, 1024, 2816], P('expert', None, 'dp'), may hold values from -0.1875 to 0.1875
- w_down: bfloat16 [16, 2816, 1024], P('expert', 'dp'), may hold values from -0.109375 to 0.109375
- cotangent: bfloat16 [4096, 1024], P(('expert', 'dp')), may hold values from -6 to 6
Outputs:
- layer_out: bfloat16 [4096, 1024], P(('expert', 'dp'))
- grad_input: float32 [4096, 1024], P(('expert', 'dp'))
- grad_norm_attn: float32 [1024], replicated
- grad_w_query: float32 [1024, 1024], replicated
- grad_w_key: float32 [1024, 1024], replicated
- grad_w_value: float32 [1024, 1024], replicated
- grad_w_out: float32 [1024, 1024], replicated
- grad_rel_table: float32 [32, 16], replicated
- grad_norm_moe: float32 [1024], replicated
- grad_router: float32 [1024, 16], replicated
- grad_w_gate: float32 [16, 1024, 2816], P('expert', None, 'dp')
- grad_w_up: float32 [16, 1024, 2816], P('expert', None, 'dp')
- grad_w_down: float32 [16, 2816, 1024], P('expert', 'dp')
Inputs may be any that keep to these rules, and one draw needn't show every extreme that they name: `routes`: each token names two different experts. `queue_slots`: A choice's place in its expert's queue within its routing group of 32 consecutive tokens, where all first choices queue before all second choices; -1 where 5 places are already taken. Within a group each place of an expert is held by at most one choice, and an expert's places are taken from 0 upward without gaps.
All inputs are finite; a program needn't handle non-finite values.
Results may differ from a plain program's by a relative error of at most 0.014.
The roundings to bfloat16 on the way count: a program that leaves them out, or rounds other values in their place, can miss the bound.
Values may be sent and summed in bfloat16 or wider, within the bound.
A program may use at most 192 MiB of HBM per device.

v0:
```python
import jax
import jax.numpy as jnp
from jax import lax
from jax.sharding import PartitionSpec as P

MICRO = 4
epsilon = 1e-06
bucket_edges = (12, 16, 23, 32, 46, 64, 91)
highest = lax.Precision.HIGHEST


def rms_scale(values):
    return lax.rsqrt(jnp.mean(values * values, axis=-1, keepdims=True) + epsilon)


def bias_block(first_row, rows_count, seq_len, rel_table):
    query_pos = first_row + jnp.arange(rows_count, dtype=jnp.int32)
    key_pos = jnp.arange(seq_len, dtype=jnp.int32)
    relative = key_pos[None, :] - query_pos[:, None]
    distance = jnp.abs(relative)
    far_bucket = jnp.full_like(distance, 8)
    for threshold in bucket_edges:
        far_bucket = far_bucket + (distance >= threshold).astype(jnp.int32)
    bucketed = jnp.where(distance < 8, distance, far_bucket) + 16 * (relative > 0).astype(jnp.int32)
    bucket_ids = jnp.arange(rel_table.shape[0], dtype=jnp.int32)
    one_hot = (bucketed[None, :, :] == bucket_ids[:, None, None]).astype(jnp.float32)
    return (one_hot, jnp.einsum("bij,bh->hij", one_hot, rel_table, precision=highest))


def attend_block(offset, query_heads, key_heads, value_heads, rel_table, block_rows):
    seq_len = key_heads.shape[0]
    one_hot, bias = bias_block(offset, block_rows, seq_len, rel_table)
    scores = (
        jnp.einsum("ihd,jhd->hij", query_heads, key_heads, preferred_element_type=jnp.float32)
        + bias
    )
    row_max = jnp.max(scores, axis=-1, keepdims=True)
    exponent = jnp.exp(scores - row_max)
    totals = jnp.sum(exponent, axis=-1, keepdims=True)
    probs_low = (exponent / totals).astype(jnp.bfloat16)
    context = jnp.einsum(
        "hij,jhd->ihd", probs_low, value_heads, preferred_element_type=jnp.float32
    ).astype(jnp.bfloat16)
    return (context, row_max[..., 0] + jnp.log(totals[..., 0]))


def gated_product(gate_pre, up_pre):
    return jax.nn.gelu(gate_pre, approximate=True) * up_pre


def expert_forward(expert_rows, gate_w, up_w):
    gate_pre = jnp.einsum("rjd,jdf->rjf", expert_rows, gate_w, preferred_element_type=jnp.float32)
    up_pre = jnp.einsum("rjd,jdf->rjf", expert_rows, up_w, preferred_element_type=jnp.float32)
    hidden = gated_product(gate_pre, up_pre).astype(jnp.bfloat16)
    return (gate_pre, up_pre, hidden)


def expert_backward(expert_rows, gate_pre, up_pre, hidden, grad_rows, gate_w, up_w, down_w):
    hidden_grad = jnp.einsum("rjd,jfd->rjf", grad_rows, down_w, preferred_element_type=jnp.float32)
    grad_down = jnp.einsum("rjf,rjd->jfd", hidden, grad_rows, preferred_element_type=jnp.float32)
    product_value, pullback = jax.vjp(gated_product, gate_pre, up_pre)
    gate_grad, up_grad = pullback(hidden_grad)
    gate_grad = gate_grad.astype(jnp.bfloat16)
    up_grad = up_grad.astype(jnp.bfloat16)
    grad_gate = jnp.einsum(
        "rjd,rjf->jdf", expert_rows, gate_grad, preferred_element_type=jnp.float32
    )
    grad_up = jnp.einsum("rjd,rjf->jdf", expert_rows, up_grad, preferred_element_type=jnp.float32)
    rows_grad = jnp.einsum("rjf,jdf->rjd", gate_grad, gate_w, preferred_element_type=jnp.float32)
    rows_grad = rows_grad + jnp.einsum(
        "rjf,jdf->rjd", up_grad, up_w, preferred_element_type=jnp.float32
    )
    return (rows_grad, grad_gate, grad_up, grad_down)


def spread_to_holders(buffer, holders, expert_groups, per_device):
    micro_count, capacity, expert_count, model_width = buffer.shape
    grouped = buffer.reshape(micro_count, capacity, expert_groups, 1, per_device, model_width)
    spread = jnp.broadcast_to(
        grouped, (micro_count, capacity, expert_groups, holders, per_device, model_width)
    )
    return spread.reshape(micro_count, capacity, expert_groups * holders * per_device, model_width)


def shards(
    layer_in,
    routes,
    queue_slots,
    norm_attn,
    w_query,
    w_key,
    w_value,
    w_out,
    rel_table,
    norm_moe,
    router,
    w_gate,
    w_up,
    w_down,
    cotangent,
):
    seq_len, model_width = layer_in.shape
    head_count = rel_table.shape[1]
    head_size = w_query.shape[1] // head_count
    expert_count = router.shape[1]
    per_device = w_gate.shape[0]
    expert_groups = lax.axis_size("expert")
    holders = lax.axis_size("dp")
    group_len = seq_len // MICRO
    capacity = (5 * group_len + 2 * expert_count - 1) // (2 * expert_count)
    block_rows = min(512, seq_len)
    block_count = seq_len // block_rows
    offsets = jnp.arange(block_count, dtype=jnp.int32) * block_rows
    split_heads = (seq_len, head_count, head_size)
    layer_rows = layer_in.astype(jnp.float32)
    inv_attn = rms_scale(layer_rows)
    normed_attn = layer_rows * inv_attn
    attn_in = (normed_attn * norm_attn).astype(jnp.bfloat16)
    queries = jnp.dot(attn_in, w_query, preferred_element_type=jnp.float32).astype(jnp.bfloat16)
    key_rows = jnp.dot(attn_in, w_key, preferred_element_type=jnp.float32).astype(jnp.bfloat16)
    value_rows = jnp.dot(attn_in, w_value, preferred_element_type=jnp.float32).astype(jnp.bfloat16)
    query_heads = queries.reshape(split_heads)
    key_heads = key_rows.reshape(split_heads)
    value_heads = value_rows.reshape(split_heads)

    def attend(offset):
        return attend_block(offset, query_heads, key_heads, value_heads, rel_table, block_rows)

    context_blocks, lse_blocks = lax.map(attend, offsets)
    context = context_blocks.reshape(seq_len, model_width)
    attn = jnp.dot(context, w_out, preferred_element_type=jnp.float32)
    residual = layer_rows + attn
    inv_moe = rms_scale(residual)
    normed_moe = residual * inv_moe
    moe_in = normed_moe * norm_moe
    logits = jnp.dot(moe_in, router, precision=highest)
    gate_prob = jax.nn.softmax(logits, axis=-1)
    expert_ids = jnp.arange(expert_count, dtype=jnp.int32)
    first_hot = (routes[:, 0:1] == expert_ids).astype(jnp.float32)
    second_hot = (routes[:, 1:2] == expert_ids).astype(jnp.float32)
    prob_first = jnp.sum(gate_prob * first_hot, axis=-1, keepdims=True)
    prob_second = jnp.sum(gate_prob * second_hot, axis=-1, keepdims=True)
    weight_first = prob_first / (prob_first + prob_second)
    weight_second = prob_second / (prob_first + prob_second)
    slot_ids = jnp.arange(capacity * expert_count, dtype=jnp.int32)
    place = queue_slots * expert_count + routes
    kept = queue_slots >= 0
    slot_shape = (MICRO, group_len, capacity * expert_count)
    select_first = (
        ((place[:, 0:1] == slot_ids) & kept[:, 0:1]).astype(jnp.bfloat16).reshape(slot_shape)
    )
    select_second = (
        ((place[:, 1:2] == slot_ids) & kept[:, 1:2]).astype(jnp.bfloat16).reshape(slot_shape)
    )
    select_both = select_first + select_second
    moe_low = moe_in.astype(jnp.bfloat16).reshape(MICRO, group_len, model_width)
    dispatched = jnp.einsum(
        "gtp,gtd->gpd", select_both, moe_low, preferred_element_type=jnp.float32
    )
    dispatched = dispatched.astype(jnp.bfloat16).reshape(MICRO, capacity, expert_count, model_width)
    spread = spread_to_holders(dispatched, holders, expert_groups, per_device)
    received = lax.all_to_all(spread, ("expert", "dp"), split_axis=2, concat_axis=0, tiled=True)
    expert_rows = received.reshape(-1, per_device, model_width)
    gate_w, up_w, down_w = (w_gate, w_up, w_down)
    gate_pre, up_pre, hidden = expert_forward(expert_rows, gate_w, up_w)
    partial_out = jnp.einsum("rjf,jfd->rjd", hidden, down_w, preferred_element_type=jnp.float32)
    partial_out = partial_out.reshape(
        expert_groups * holders * MICRO, capacity, per_device, model_width
    )
    returned_out = lax.all_to_all(
        partial_out.astype(jnp.bfloat16), ("expert", "dp"), split_axis=0, concat_axis=2, tiled=True
    ).astype(partial_out.dtype)
    returned_out = returned_out.reshape(
        MICRO, capacity, expert_groups, holders, per_device, model_width
    )
    expert_out = (
        jnp.sum(returned_out, axis=3)
        .astype(jnp.bfloat16)
        .reshape(MICRO, capacity * expert_count, model_width)
    )
    picked_first = jnp.einsum(
        "gtp,gpd->gtd", select_first, expert_out, preferred_element_type=jnp.float32
    ).reshape(seq_len, model_width)
    picked_second = jnp.einsum(
        "gtp,gpd->gtd", select_second, expert_out, preferred_element_type=jnp.float32
    ).reshape(seq_len, model_width)
    moe = weight_first * picked_first + weight_second * picked_second
    layer_out = (residual + moe).astype(jnp.bfloat16)
    cot_rows = cotangent.astype(jnp.float32)
    grad_weight_first = jnp.sum(cot_rows * picked_first, axis=-1, keepdims=True)
    grad_weight_second = jnp.sum(cot_rows * picked_second, axis=-1, keepdims=True)
    sent_first = (
        (weight_first * cot_rows).astype(jnp.bfloat16).reshape(MICRO, group_len, model_width)
    )
    sent_second = (
        (weight_second * cot_rows).astype(jnp.bfloat16).reshape(MICRO, group_len, model_width)
    )
    grad_expert_out = jnp.einsum(
        "gtp,gtd->gpd", select_first, sent_first, preferred_element_type=jnp.float32
    )
    grad_expert_out = grad_expert_out + jnp.einsum(
        "gtp,gtd->gpd", select_second, sent_second, preferred_element_type=jnp.float32
    )
    grad_expert_out = grad_expert_out.astype(jnp.bfloat16).reshape(
        MICRO, capacity, expert_count, model_width
    )
    grad_spread = spread_to_holders(grad_expert_out, holders, expert_groups, per_device)
    grad_received = lax.all_to_all(
        grad_spread, ("expert", "dp"), split_axis=2, concat_axis=0, tiled=True
    )
    grad_rows = grad_received.reshape(-1, per_device, model_width)
    rows_grad, grad_w_gate, grad_w_up, grad_w_down = expert_backward(
        expert_rows, gate_pre, up_pre, hidden, grad_rows, gate_w, up_w, down_w
    )
    rows_grad = rows_grad.reshape(
        expert_groups * holders * MICRO, capacity, per_device, model_width
    )
    grad_returned = lax.all_to_all(
        rows_grad.astype(jnp.bfloat16), ("expert", "dp"), split_axis=0, concat_axis=2, tiled=True
    ).astype(rows_grad.dtype)
    grad_returned = grad_returned.reshape(
        MICRO, capacity, expert_groups, holders, per_device, model_width
    )
    grad_dispatched = (
        jnp.sum(grad_returned, axis=3)
        .astype(jnp.bfloat16)
        .reshape(MICRO, capacity * expert_count, model_width)
    )
    grad_from_slots = jnp.einsum(
        "gtp,gpd->gtd", select_both, grad_dispatched, preferred_element_type=jnp.float32
    )
    grad_from_slots = grad_from_slots.reshape(seq_len, model_width)
    mean_grad = weight_first * grad_weight_first + weight_second * grad_weight_second
    logit_first = weight_first * (grad_weight_first - mean_grad)
    logit_second = weight_second * (grad_weight_second - mean_grad)
    grad_logits = logit_first * first_hot + logit_second * second_hot
    grad_router = jnp.einsum("sd,se->de", moe_in, grad_logits, precision=highest)
    grad_moe_in = grad_from_slots + jnp.einsum("se,de->sd", grad_logits, router, precision=highest)
    grad_norm_moe = jnp.sum(grad_moe_in * normed_moe, axis=0)
    grad_normed = grad_moe_in * norm_moe
    grad_residual = cot_rows + inv_moe * (
        grad_normed - normed_moe * jnp.mean(grad_normed * normed_moe, axis=-1, keepdims=True)
    )
    grad_attn_low = grad_residual.astype(jnp.bfloat16)
    grad_w_out = jnp.einsum("se,sd->ed", context, grad_attn_low, preferred_element_type=jnp.float32)
    grad_context = jnp.einsum(
        "sd,ed->se", grad_attn_low, w_out, preferred_element_type=jnp.float32
    ).astype(jnp.bfloat16)
    grad_context_heads = grad_context.reshape(split_heads)

    def attend_back(totals, block_in):
        grad_keys_acc, grad_values_acc, grad_table = totals
        offset, lse_block = block_in
        one_hot, bias = bias_block(offset, block_rows, seq_len, rel_table)
        scores = (
            jnp.einsum("ihd,jhd->hij", query_heads, key_heads, preferred_element_type=jnp.float32)
            + bias
        )
        attn_probs = jnp.exp(scores - lse_block[:, :, None])
        probs_low = attn_probs.astype(jnp.bfloat16)
        grad_values_acc = grad_values_acc + jnp.einsum(
            "hij,ihd->jhd", probs_low, grad_context_heads, preferred_element_type=jnp.float32
        )
        grad_probs = jnp.einsum(
            "ihd,jhd->hij", grad_context_heads, value_heads, preferred_element_type=jnp.float32
        )
        grad_scores = attn_probs * (
            grad_probs - jnp.sum(attn_probs * grad_probs, axis=-1, keepdims=True)
        )
        grad_table = grad_table + jnp.einsum("bij,hij->bh", one_hot, grad_scores, precision=highest)
        scores_low = grad_scores.astype(jnp.bfloat16)
        grad_query_blk = jnp.einsum(
            "hij,jhd->ihd", scores_low, key_heads, preferred_element_type=jnp.float32
        ).astype(jnp.bfloat16)
        grad_keys_acc = grad_keys_acc + jnp.einsum(
            "hij,ihd->jhd", scores_low, query_heads, preferred_element_type=jnp.float32
        )
        return ((grad_keys_acc, grad_values_acc, grad_table), grad_query_blk)

    start_totals = (
        jnp.zeros(split_heads, jnp.float32),
        jnp.zeros(split_heads, jnp.float32),
        jnp.zeros(rel_table.shape, jnp.float32),
    )
    end_totals, grad_query_blocks = lax.scan(attend_back, start_totals, (offsets, lse_blocks))
    grad_keys_acc, grad_values_acc, grad_rel_table = end_totals
    grad_queries = grad_query_blocks.reshape(seq_len, model_width)
    grad_keys = grad_keys_acc.reshape(seq_len, model_width).astype(jnp.bfloat16)
    grad_values = grad_values_acc.reshape(seq_len, model_width).astype(jnp.bfloat16)
    grad_w_query = jnp.einsum(
        "sd,se->de", attn_in, grad_queries, preferred_element_type=jnp.float32
    )
    grad_w_key = jnp.einsum("sd,se->de", attn_in, grad_keys, preferred_element_type=jnp.float32)
    grad_w_value = jnp.einsum("sd,se->de", attn_in, grad_values, preferred_element_type=jnp.float32)
    grad_attn_in = jnp.einsum(
        "se,de->sd", grad_queries, w_query, preferred_element_type=jnp.float32
    )
    grad_attn_in = grad_attn_in + jnp.einsum(
        "se,de->sd", grad_keys, w_key, preferred_element_type=jnp.float32
    )
    grad_attn_in = grad_attn_in + jnp.einsum(
        "se,de->sd", grad_values, w_value, preferred_element_type=jnp.float32
    )
    grad_norm_attn = jnp.sum(grad_attn_in * normed_attn, axis=0)
    grad_normed_attn = grad_attn_in * norm_attn
    grad_input = grad_residual + inv_attn * (
        grad_normed_attn
        - normed_attn * jnp.mean(grad_normed_attn * normed_attn, axis=-1, keepdims=True)
    )
    summed = lax.psum(
        (
            grad_norm_attn,
            grad_w_query,
            grad_w_key,
            grad_w_value,
            grad_w_out,
            grad_rel_table,
            grad_norm_moe,
            grad_router,
        ),
        ("expert", "dp"),
    )
    return (
        layer_out,
        grad_input,
        summed[0],
        summed[1],
        summed[2],
        summed[3],
        summed[4],
        summed[5],
        summed[6],
        summed[7],
        grad_w_gate,
        grad_w_up,
        grad_w_down,
    )


def solution(mesh):
    in_specs = (
        P(("expert", "dp"), None),
        P(("expert", "dp"), None),
        P(("expert", "dp"), None),
        P(),
        P(),
        P(),
        P(),
        P(),
        P(),
        P(),
        P(),
        P("expert", None, "dp"),
        P("expert", None, "dp"),
        P("expert", "dp", None),
        P(("expert", "dp"), None),
    )
    out_specs = (
        P(("expert", "dp"), None),
        P(("expert", "dp"), None),
        P(),
        P(),
        P(),
        P(),
        P(),
        P(),
        P(),
        P(),
        P("expert", None, "dp"),
        P("expert", None, "dp"),
        P("expert", "dp", None),
    )
    return jax.shard_map(shards, mesh=mesh, in_specs=in_specs, out_specs=out_specs, check_vma=False)
```

profile of v0, /device:TPU:0, one launch (start us, length us, event | category | flops | bytes accessed | tf_op | source)
XLA Modules:
  0.0 683.5 jit_solution(15179382950645383366)
XLA Ops:
  13.3 2.5 copy.91
  15.9 2.8 convolution_convert_fusion.7
  19.8 2.8 convolution_convert_fusion.6
  32.6 2.6 broadcast_in_dim.46
  38.1 67.6 %all_to_all.48 = bf16[4,5,64,1024]{3,0,1,2:T(4,128)(2,1)S(1)} all-to-all(bf16[4,5,64,1024]{3,0,1,2:T(4,128)(2,1)S(1)} %bitcast.150), channel_id=1, replica_groups=mesh['expert'=8,'dp'=4] {'expert','dp'}, dimensions={2} | all-to-all | bytes 5242880 | tf_op jit(solution)/shard_map/all_to_all | solution.py:162
  105.7 2.6 copy.95
  108.4 2.5 fusion.24
  111.1 4.9 fusion.8
  119.6 4.6 copy.98
  124.2 3.7 all-to-all-start.1
  131.4 56.6 %all-to-all-done.1 = bf16[128,5,2,1024]{3,2,1,0:T(2,128)(2,1)} async-done(((bf16[128,5,2,1024]{3,2,1,0:T(2,128)(2,1)}), bf16[128,5,2,1024]{3,2,1,0:T(2,128)(2,1)}, u32[]{:S(2)}, u32[]{:S(2)}) %all-to-all-start.1) | async-done | bytes 2621472 | tf_op jit(solution)/shard_map/all_to_all | solution.py:170
  188.1 6.2 reduce
  201.4 2.6 broadcast_in_dim.48
  206.9 64.7 %all_to_all.49 = bf16[4,5,64,1024]{3,0,1,2:T(4,128)(2,1)S(1)} all-to-all(bf16[4,5,64,1024]{3,0,1,2:T(4,128)(2,1)S(1)} %bitcast.152), channel_id=1, replica_groups=mesh['expert'=8,'dp'=4] {'expert','dp'}, dimensions={2} | all-to-all | bytes 5242880 | tf_op jit(solution)/shard_map/all_to_all | solution.py:208
  271.6 2.6 copy.104
  274.3 5.0 fusion.7
  284.7 4.2 copy.106
  289.0 3.7 all-to-all-start.3
  294.2 58.7 %all-to-all-done.3 = bf16[128,5,2,1024]{3,2,1,0:T(2,128)(2,1)} async-done(((bf16[128,5,2,1024]{3,2,1,0:T(2,128)(2,1)}), bf16[128,5,2,1024]{3,2,1,0:T(2,128)(2,1)}, u32[]{:S(2)}, u32[]{:S(2)}) %all-to-all-start.3) | async-done | bytes 2621472 | tf_op jit(solution)/shard_map/all_to_all | solution.py:218
  352.9 5.4 reduce.1
  365.1 2.7 fusion.70
  367.8 2.8 fusion.122
  370.6 2.8 fusion.120
  373.4 2.8 fusion.118
  376.3 7.7 %fusion.18 = f32[2,1024,704]{1,2,0:T(8,128)} fusion(bf16[640,2,704]{0,2,1:T(8,128)(2,1)} %copy-done.88, bf16[640,2,1024]{2,1,0:T(2,128)(2,1)} %bitcast.158), kind=kOutput, calls=%fused_computation.28 | convolution fusion | flops 1845493760 | bytes 10190848 | tf_op jit(solution)/shard_map/rjd,rjf->jdf/dot_general | solution.py:65
  384.0 5.0 fusion.20
  389.0 5.0 fusion.12
  395.4 2.6 fusion.27
  397.9 2.7 fusion.130
  402.5 40.2 %all-reduce = (f32[1024]{0:T(1024)}, f32[32,16]{0,1:T(8,128)}, f32[1024]{0:T(1024)}) all-reduce(f32[1024]{0:T(1024)S(1)} %get-tuple-element.58, f32[32,16]{0,1:T(8,128)S(1)} %fusion.27, f32[1024]{0:T(1024)S(1)} %copy-done.50), channel_id=1, replica_groups=mesh['expert'=8,'dp'=4] {'expert','dp'}, use_global_device_ids=true, to_apply=%region_16.17 | all-reduce | flops 2560 | bytes 20480 | tf_op jit(solution)/shard_map/psum | solution.py:310
  443.7 217.5 %all-reduce.4.cloned.1.call-done = (f32[1024,1024]{1,0:T(8,128)}, f32[1024,1024]{1,0:T(8,128)}, f32[1024,1024]{1,0:T(8,128)}, f32[1024,1024]{1,0:T(8,128)}, f32[1024,16]{0,1:T(8,128)}) async-done(((f32[1024,1024]{1,0:T(8,128)}, f32[1024,1024]{1,0:T(8,128)}, f32[1024,1024]{1,0:T(8,128)}, f32[1024,1024]{1,0:T(8,128)}, f32[1024,16]{0,1:T(8,128)}), (f32[1024,1024]{1,0:T(8,128)}, f32[1024,1024]{1,0:T(8,128)}, ...) | async-done | bytes 16842768 | tf_op jit(solution)/shard_map/psum | solution.py:310
  661.2 4.9 copy.150
  (252 shorter events, 65.0 us)
Async XLA Ops:
  7.2 110.1 %copy-start = (bf16[2,704,1024]{2,1,0:T(8,128)(2,1)S(1)}, bf16[2,704,1024]{2,1,0:T(8,128)(2,1)}, u32[]{:S(2)}) copy-start(bf16[2,704,1024]{2,1,0:T(8,128)(2,1)} %param.28) | copy-start | bytes 8650756
  8.5 11.3 %copy-start.48 = (f32[128]{0:T(128)}, f32[128]{0:T(128)S(1)}, u32[]{:S(2)}) copy-start(f32[128]{0:T(128)S(1)} %add_rsqrt_fusion.1) | copy-start | bytes 1540
  8.5 7.4 %copy-start.4 = (bf16[128,1024]{1,0:T(8,128)(2,1)S(1)}, bf16[128,1024]{1,0:T(8,128)(2,1)}, u32[]{:S(2)}) copy-start(bf16[128,1024]{1,0:T(8,128)(2,1)} %param.15) | copy-start | bytes 786436
  8.5 7.4 %copy-start.35 = (f32[1024]{0:T(1024)S(1)}, f32[1024]{0:T(1024)}, u32[]{:S(2)}) copy-start(f32[1024]{0:T(1024)} %param.18) | copy-start | bytes 12292
  29.5 8.6 %copy-start.51 = (f32[128]{0:T(128)}, f32[128]{0:T(128)S(1)}, u32[]{:S(2)}) copy-start(f32[128]{0:T(128)S(1)} %add_rsqrt_fusion) | copy-start | bytes 1540
  29.7 8.4 %copy-start.43 = (s32[4,32]{1,0:T(4,128)}, s32[4,32]{1,0:T(4,128)S(1)}, u32[]{:S(2)}) copy-start(s32[4,32]{1,0:T(4,128)S(1)} %eq.119) | copy-start | bytes 1540
  29.8 8.3 %copy-start.40 = (s32[4,32]{1,0:T(4,128)}, s32[4,32]{1,0:T(4,128)S(1)}, u32[]{:S(2)}) copy-start(s32[4,32]{1,0:T(4,128)S(1)} %eq.115) | copy-start | bytes 1540
  29.9 8.2 %copy-start.62 = (pred[4,32]{1,0:T(4,128)(4,1)}, pred[4,32]{1,0:T(4,128)(4,1)S(1)}, u32[]{:S(2)}) copy-start(pred[4,32]{1,0:T(4,128)(4,1)S(1)} %and.27) | copy-start | bytes 388
  30.0 8.2 %copy-start.55 = (pred[4,32]{1,0:T(4,128)(4,1)}, pred[4,32]{1,0:T(4,128)(4,1)S(1)}, u32[]{:S(2)}) copy-start(pred[4,32]{1,0:T(4,128)(4,1)S(1)} %and.24) | copy-start | bytes 388
  111.1 4.9 copy-start.89
  124.2 63.9 %all-to-all-start.1 = ((bf16[128,5,2,1024]{3,2,1,0:T(2,128)(2,1)}), bf16[128,5,2,1024]{3,2,1,0:T(2,128)(2,1)}, u32[]{:S(2)}, u32[]{:S(2)}) async-start(bf16[128,5,2,1024]{3,2,1,0:T(2,128)(2,1)} %bitcast.148), calls=%async_computation.1 | async-start | bytes 5242880 | tf_op jit(solution)/shard_map/all_to_all | solution.py:170
  188.1 8.9 %copy-start.44 = (s32[4,32]{1,0:T(4,128)S(1)}, s32[4,32]{1,0:T(4,128)}, u32[]{:S(2)}) copy-start(s32[4,32]{1,0:T(4,128)} %copy-done.43) | copy-start | bytes 1540
  194.3 5.2 copy-start.41
  194.3 5.2 copy-start.56
  206.9 67.3 %copy-start.91 = (f32[2,640,704]{1,2,0:T(8,128)S(1)}, f32[2,640,704]{1,2,0:T(8,128)}, u32[]{:S(2)}) copy-start(f32[2,640,704]{1,2,0:T(8,128)} %get-tuple-element.103) | copy-start | bytes 10813444
  274.2 5.0 copy-start.19
  274.2 5.0 copy-start.81
  289.0 63.9 %all-to-all-start.3 = ((bf16[128,5,2,1024]{3,2,1,0:T(2,128)(2,1)}), bf16[128,5,2,1024]{3,2,1,0:T(2,128)(2,1)}, u32[]{:S(2)}, u32[]{:S(2)}) async-start(bf16[128,5,2,1024]{3,2,1,0:T(2,128)(2,1)} %bitcast.149), calls=%async_computation.3 | async-start | bytes 5242880 | tf_op jit(solution)/shard_map/all_to_all | solution.py:218
  292.7 66.0 %copy-start.42 = (s32[4,32]{1,0:T(4,128)S(1)}, s32[4,32]{1,0:T(4,128)}, u32[]{:S(2)}) copy-start(s32[4,32]{1,0:T(4,128)} %copy-done.40) | copy-start | bytes 1540
  292.7 66.0 %copy-start.45 = (s32[4,32]{1,0:T(4,128)S(1)}, s32[4,32]{1,0:T(4,128)}, u32[]{:S(2)}) copy-start(s32[4,32]{1,0:T(4,128)} %copy-done.43) | copy-start | bytes 1540
  292.7 66.0 %copy-start.57 = (pred[4,32]{1,0:T(4,128)(4,1)S(1)}, pred[4,32]{1,0:T(4,128)(4,1)}, u32[]{:S(2)}) copy-start(pred[4,32]{1,0:T(4,128)(4,1)} %copy-done.55) | copy-start | bytes 388
  292.7 66.0 %copy-start.64 = (pred[4,32]{1,0:T(4,128)(4,1)S(1)}, pred[4,32]{1,0:T(4,128)(4,1)}, u32[]{:S(2)}) copy-start(pred[4,32]{1,0:T(4,128)(4,1)} %copy-done.62) | copy-start | bytes 388
  292.7 368.5 %all-reduce.4.cloned.1.call-start = ((), (), s32[]{:S(2)}) async-start(), calls=%async_computation.4 | async-start | bytes 33685504 | tf_op jit(solution)/shard_map/psum | solution.py:310
  364.5 6.0 copy-start.26
  376.3 7.7 %copy-start.18 = (bf16[32,4,5,2,1024]{4,3,2,1,0:T(2,128)(2,1)S(1)}, bf16[32,4,5,2,1024]{4,3,2,1,0:T(2,128)(2,1)}, u32[]{:S(2)}) copy-start(bf16[32,4,5,2,1024]{4,3,2,1,0:T(2,128)(2,1)} %copy-done.17) | copy-start | bytes 7864324
  376.3 7.7 %copy-start.87 = (bf16[640,2,704]{0,2,1:T(8,128)(2,1)S(1)}, bf16[640,2,704]{0,2,1:T(8,128)(2,1)}, u32[]{:S(2)}) copy-start(bf16[640,2,704]{0,2,1:T(8,128)(2,1)} %copy-done.86) | copy-start | bytes 5406724
  384.0 5.0 copy-start.20
  384.0 5.0 copy-start.85
  395.4 5.3 copy-start.8
  395.4 5.3 copy-start.27
  661.2 4.9 copy-start.16
  669.9 6.4 copy-start.1
  (63 other events, 172.1 us)
Sparse Core Ops, SparseCore 0:
  376.4 284.7 all-reduce.3
where the time goes:
time: 690 us; the launch traced here: 683 us
  waiting for transfers between devices  333 us (48%)
  blocking collectives  172 us (25%)
  matrix products  80.5 us (12%)
  local copies, waits for them, and re-layouts  56.4 us (8%)
  other arithmetic  18 us (3%)
  between operations  15.7 us (2%)
  starting transfers between devices  7.59 us (1%)
    psum x1, waiting for transfers between devices, shards(): lax.psum((grad_norm_attn, grad_w_query, grad_w_key, grad_w_value, grad_w_...  217 us
    all_to_all x1, blocking collectives, shards(): lax.all_to_all(spread, ('expert', 'dp'), split_axis=2, concat_axis=0, til...  67.6 us
    all_to_all x1, blocking collectives, shards(): lax.all_to_all(grad_spread, ('expert', 'dp'), split_axis=2, concat_axis=0...  64.7 us
    all_to_all x1, waiting for transfers between devices, shards(): lax.all_to_all(rows_grad.astype(jnp.bfloat16), ('expert', 'dp'), split_ax...  58.7 us
    all_to_all x1, waiting for transfers between devices, shards(): lax.all_to_all(partial_out.astype(jnp.bfloat16), ('expert', 'dp'), split_...  56.6 us
    psum x1, blocking collectives, shards(): lax.psum((grad_norm_attn, grad_w_query, grad_w_key, grad_w_value, grad_w_...  40.2 us
    unnamed x189, local copies, waits for them, and re-layouts  20.6 us
  transfers between devices with their start and end apart: 3, of which 3 were waited for; matrix products, arithmetic and copies ran while one was open for 5% of the time, Pallas kernels for 0%

commit v1 on v0

--- a/solution.py
+++ b/solution.py
@@ -308,17 +308,20 @@
         - normed_attn * jnp.mean(grad_normed_attn * normed_attn, axis=-1, keepdims=True)
     )
     summed = lax.psum(
-        (
-            grad_norm_attn,
-            grad_w_query,
-            grad_w_key,
-            grad_w_value,
-            grad_w_out,
-            grad_rel_table,
-            grad_norm_moe,
-            grad_router,
+        lax.psum(
+            (
+                grad_norm_attn,
+                grad_w_query,
+                grad_w_key,
+                grad_w_value,
+                grad_w_out,
+                grad_rel_table,
+                grad_norm_moe,
+                grad_router,
+            ),
+            "dp",
         ),
-        ("expert", "dp"),
+        "expert",
     )
     return (
         layer_out,

time: 690 us -> 1220 us (1.77)
  waiting for transfers between devices: 333 us -> 851 us
    psum x0 -> x1, waiting for transfers between devices: none -> 444 us  [shards(): lax.psum(lax.psum((grad_norm_attn, grad_w_query, grad_w_key, grad_w_value...]
    psum x1, waiting for transfers between devices: 217 us -> 291 us  [shards(): lax.psum((grad_norm_attn, grad_w_query, grad_w_key, grad_w_value, grad_w_...]
    psum x0 -> x1, blocking collectives: none -> 40.2 us  [shards(): lax.psum(lax.psum((grad_norm_attn, grad_w_query, grad_w_key, grad_w_value...]
    psum x1, blocking collectives: 40.2 us -> 11 us  [shards(): lax.psum((grad_norm_attn, grad_w_query, grad_w_key, grad_w_value, grad_w_...]
  transfers between devices with their start and end apart: 3 -> 4, of which waited for: 3 -> 4; matrix products, arithmetic and copies ran while one was open for 5% -> 3% of each run, Pallas kernels for 0% -> 0%
where the time goes in v1:
time: 1220 us; the launch traced here: 1210 us
  waiting for transfers between devices  851 us (70%)
  blocking collectives  183 us (15%)
  matrix products  80.7 us (7%)
  local copies, waits for them, and re-layouts  56.3 us (5%)
  other arithmetic  18 us (1%)
  between operations  15.7 us (1%)
    psum x1, waiting for transfers between devices, shards(): lax.psum(lax.psum((grad_norm_attn, grad_w_query, grad_w_key, grad_w_value...  444 us
    psum x1, waiting for transfers between devices, shards(): lax.psum((grad_norm_attn, grad_w_query, grad_w_key, grad_w_value, grad_w_...  291 us
    all_to_all x1, blocking collectives, shards(): lax.all_to_all(spread, ('expert', 'dp'), split_axis=2, concat_axis=0, til...  67.6 us
    all_to_all x1, blocking collectives, shards(): lax.all_to_all(grad_spread, ('expert', 'dp'), split_axis=2, concat_axis=0...  64.7 us
    all_to_all x1, waiting for transfers between devices, shards(): lax.all_to_all(rows_grad.astype(jnp.bfloat16), ('expert', 'dp'), split_ax...  58.9 us
    all_to_all x1, waiting for transfers between devices, shards(): lax.all_to_all(partial_out.astype(jnp.bfloat16), ('expert', 'dp'), split_...  56.6 us
    psum x1, blocking collectives, shards(): lax.psum(lax.psum((grad_norm_attn, grad_w_query, grad_w_key, grad_w_value...  40.2 us
  transfers between devices with their start and end apart: 4, of which 4 were waited for; matrix products, arithmetic and copies ran while one was open for 3% of the time, Pallas kernels for 0%

profile of v1, /device:TPU:0, one launch (start us, length us, event | category | flops | bytes accessed | tf_op | source)
XLA Modules:
  0.0 1212.8 jit_solution(5618591154919555863)
XLA Ops:
  13.3 2.5 copy.91
  15.9 2.8 convolution_convert_fusion.7
  19.8 2.8 convolution_convert_fusion.6
  32.6 2.6 broadcast_in_dim.46
  38.1 67.6 %all_to_all.48 = bf16[4,5,64,1024]{3,0,1,2:T(4,128)(2,1)S(1)} all-to-all(bf16[4,5,64,1024]{3,0,1,2:T(4,128)(2,1)S(1)} %bitcast.150), channel_id=1, replica_groups=mesh['expert'=8,'dp'=4] {'expert','dp'}, dimensions={2} | all-to-all | bytes 5242880 | tf_op jit(solution)/shard_map/all_to_all | solution.py:162
  105.7 2.6 copy.95
  111.1 4.9 fusion.8
  119.5 4.6 copy.98
  124.1 3.7 all-to-all-start.1
  131.4 56.6 %all-to-all-done.1 = bf16[128,5,2,1024]{3,2,1,0:T(2,128)(2,1)} async-done(((bf16[128,5,2,1024]{3,2,1,0:T(2,128)(2,1)}), bf16[128,5,2,1024]{3,2,1,0:T(2,128)(2,1)}, u32[]{:S(2)}, u32[]{:S(2)}) %all-to-all-start.1) | async-done | bytes 2621472 | tf_op jit(solution)/shard_map/all_to_all | solution.py:170
  188.1 6.2 reduce
  201.4 2.6 broadcast_in_dim.48
  206.9 64.7 %all_to_all.49 = bf16[4,5,64,1024]{3,0,1,2:T(4,128)(2,1)S(1)} all-to-all(bf16[4,5,64,1024]{3,0,1,2:T(4,128)(2,1)S(1)} %bitcast.152), channel_id=1, replica_groups=mesh['expert'=8,'dp'=4] {'expert','dp'}, dimensions={2} | all-to-all | bytes 5242880 | tf_op jit(solution)/shard_map/all_to_all | solution.py:208
  271.6 2.6 copy.104
  274.2 5.0 fusion.7
  284.7 4.2 copy.106
  289.0 3.9 all-to-all-start.3
  294.2 58.9 %all-to-all-done.3 = bf16[128,5,2,1024]{3,2,1,0:T(2,128)(2,1)} async-done(((bf16[128,5,2,1024]{3,2,1,0:T(2,128)(2,1)}), bf16[128,5,2,1024]{3,2,1,0:T(2,128)(2,1)}, u32[]{:S(2)}, u32[]{:S(2)}) %all-to-all-start.3) | async-done | bytes 2621472 | tf_op jit(solution)/shard_map/all_to_all | solution.py:218
  353.1 5.4 reduce.1
  365.3 2.7 fusion.70
  368.0 2.8 fusion.122
  370.8 2.8 fusion.120
  373.6 2.8 fusion.118
  376.8 291.3 %all-reduce.9.cloned.1.call-done = (f32[1024,1024]{1,0:T(8,128)}, f32[1024,1024]{1,0:T(8,128)}, f32[1024,1024]{1,0:T(8,128)}, f32[1024,1024]{1,0:T(8,128)}, f32[1024,16]{0,1:T(8,128)}) async-done(((f32[1024,1024]{1,0:T(8,128)}, f32[1024,1024]{1,0:T(8,128)}, f32[1024,1024]{1,0:T(8,128)}, f32[1024,1024]{1,0:T(8,128)}, f32[1024,16]{0,1:T(8,128)}), (f32[1024,1024]{1,0:T(8,128)}, f32[1024,1024]{1,0:T(8,128)}, ...) | async-done | bytes 16842768 | tf_op jit(solution)/shard_map/psum | solution.py:311
  668.1 7.4 fusion.18
  675.6 5.6 fusion.20
  681.1 5.0 fusion.12
  690.0 2.6 fusion.130
  694.5 11.0 all-reduce.2
  705.5 40.2 %all-reduce = (f32[1024]{0:T(1024)}, f32[32,16]{0,1:T(8,128)}, f32[1024]{0:T(1024)}) all-reduce(f32[1024]{0:T(1024)S(1)} %get-tuple-element.87, f32[32,16]{0,1:T(8,128)S(1)} %get-tuple-element.88, f32[1024]{0:T(1024)S(1)} %get-tuple-element.89), channel_id=1, replica_groups=mesh['expert'=8,'dp'=4] {'expert'}, use_global_device_ids=true, to_apply=%region_17.18 | all-reduce | flops 2560 | bytes 20480 | tf_op jit(solution)/shard_map/psum | solution.py:310
  746.7 443.8 %all-reduce.7.cloned.1.call-done = (f32[1024,1024]{1,0:T(8,128)}, f32[1024,1024]{1,0:T(8,128)}, f32[1024,1024]{1,0:T(8,128)}, f32[1024,1024]{1,0:T(8,128)}, f32[1024,16]{0,1:T(8,128)}) async-done(((f32[1024,1024]{1,0:T(8,128)}, f32[1024,1024]{1,0:T(8,128)}, f32[1024,1024]{1,0:T(8,128)}, f32[1024,1024]{1,0:T(8,128)}, f32[1024,16]{0,1:T(8,128)}), (f32[1024,1024]{1,0:T(8,128)}, f32[1024,1024]{1,0:T(8,128)}, ...) | async-done | bytes 16842768 | tf_op jit(solution)/shard_map/psum | solution.py:310
  1190.6 4.9 copy.155
  (256 shorter events, 70.0 us)
Async XLA Ops:
  7.2 110.1 %copy-start = (bf16[2,704,1024]{2,1,0:T(8,128)(2,1)S(1)}, bf16[2,704,1024]{2,1,0:T(8,128)(2,1)}, u32[]{:S(2)}) copy-start(bf16[2,704,1024]{2,1,0:T(8,128)(2,1)} %param.28) | copy-start | bytes 8650756
  8.5 11.3 copy-start.48
  8.5 7.4 copy-start.4
  8.5 7.4 copy-start.35
  29.5 8.6 copy-start.51
  29.7 8.4 copy-start.43
  29.8 8.3 copy-start.40
  29.9 8.2 copy-start.62
  30.0 8.2 copy-start.55
  124.1 63.9 %all-to-all-start.1 = ((bf16[128,5,2,1024]{3,2,1,0:T(2,128)(2,1)}), bf16[128,5,2,1024]{3,2,1,0:T(2,128)(2,1)}, u32[]{:S(2)}, u32[]{:S(2)}) async-start(bf16[128,5,2,1024]{3,2,1,0:T(2,128)(2,1)} %bitcast.148), calls=%async_computation.1 | async-start | bytes 5242880 | tf_op jit(solution)/shard_map/all_to_all | solution.py:170
  188.1 8.9 copy-start.44
  194.3 5.2 copy-start.41
  194.3 5.2 copy-start.56
  206.9 67.3 %copy-start.91 = (f32[2,640,704]{1,2,0:T(8,128)S(1)}, f32[2,640,704]{1,2,0:T(8,128)}, u32[]{:S(2)}) copy-start(f32[2,640,704]{1,2,0:T(8,128)} %get-tuple-element.111) | copy-start | bytes 10813444
  274.2 5.0 copy-start.19
  274.2 5.0 copy-start.81
  289.0 64.1 %all-to-all-start.3 = ((bf16[128,5,2,1024]{3,2,1,0:T(2,128)(2,1)}), bf16[128,5,2,1024]{3,2,1,0:T(2,128)(2,1)}, u32[]{:S(2)}, u32[]{:S(2)}) async-start(bf16[128,5,2,1024]{3,2,1,0:T(2,128)(2,1)} %bitcast.149), calls=%async_computation.3 | async-start | bytes 5242880 | tf_op jit(solution)/shard_map/all_to_all | solution.py:218
  292.9 66.0 %copy-start.42 = (s32[4,32]{1,0:T(4,128)S(1)}, s32[4,32]{1,0:T(4,128)}, u32[]{:S(2)}) copy-start(s32[4,32]{1,0:T(4,128)} %copy-done.40) | copy-start | bytes 1540
  292.9 66.0 %copy-start.45 = (s32[4,32]{1,0:T(4,128)S(1)}, s32[4,32]{1,0:T(4,128)}, u32[]{:S(2)}) copy-start(s32[4,32]{1,0:T(4,128)} %copy-done.43) | copy-start | bytes 1540
  292.9 66.0 %copy-start.57 = (pred[4,32]{1,0:T(4,128)(4,1)S(1)}, pred[4,32]{1,0:T(4,128)(4,1)}, u32[]{:S(2)}) copy-start(pred[4,32]{1,0:T(4,128)(4,1)} %copy-done.55) | copy-start | bytes 388
  292.9 66.0 %copy-start.64 = (pred[4,32]{1,0:T(4,128)(4,1)S(1)}, pred[4,32]{1,0:T(4,128)(4,1)}, u32[]{:S(2)}) copy-start(pred[4,32]{1,0:T(4,128)(4,1)} %copy-done.62) | copy-start | bytes 388
  292.9 375.2 %all-reduce.9.cloned.1.call-start = ((), (), s32[]{:S(2)}) async-start(), calls=%async_computation.5 | async-start | bytes 33685504 | tf_op jit(solution)/shard_map/psum | solution.py:311
  364.7 6.0 copy-start.26
  376.5 814.1 %all-reduce.7.cloned.1.call-start = ((), (), s32[]{:S(2)}) async-start(), calls=%async_computation.4 | async-start | bytes 33685504 | tf_op jit(solution)/shard_map/psum | solution.py:310
  668.1 7.4 copy-start.18
  668.1 7.4 copy-start.87
  675.5 5.6 copy-start.20
  675.5 5.6 copy-start.85
  687.5 5.1 copy-start.8
  687.5 5.2 copy-start.27
  1190.5 4.9 copy-start.16
  1199.2 6.4 copy-start.1
  (64 other events, 176.8 us)
Sparse Core Ops, SparseCore 0:
  376.6 291.4 all-reduce.8
  673.2 517.2 all-reduce.6
